TPU v7x, 256 devices: a whole 4x4x8 slice. The times are simulated.
256 devices in a mesh: pole: 4 (over y), row: 8 (over z), col: 8 (over x, core).
Axes of the slice: x: 4, y: 4, z: 8, core: 2. Of those that a mesh axis runs over, the one named last changes fastest.
Arguments:
- root_inverse: float32 [8, 1024, 1024], P('pole', ('row', 'col')), may hold values from -100 to 100
- node_factor: float32 [8, 8, 1024, 512], P('pole', 'row', None, 'col'), may hold values from -0.1875 to 0.1875
- node_inverse: float32 [8, 8, 512, 512], P('pole', 'row'), may hold values from -100 to 100
- leaf_root_factor: float32 [8, 64, 1024, 256], P('pole', ('row', 'col')), may hold values from -0.1875 to 0.1875
- leaf_node_factor: float32 [8, 64, 512, 256], P('pole', ('row', 'col')), may hold values from -0.25 to 0.25
- leaf_inverse: float32 [8, 64, 256, 256], P('pole', ('row', 'col')), may hold values from -100 to 100
- leaf_pattern: int32 [64, 8], P(('row', 'col')), may hold values 0 or 1
- pole_weight: float32 [8], P('pole'), may hold values from 0.1 to 1
Outputs:
- root_block: float32 [1024, 1024], P(('row', 'col'))
- node_offdiag: float32 [8, 1024, 512], P('row', None, 'col')
- node_diag: float32 [8, 512, 512], P('row', 'col')
- leaf_root: float32 [64, 1024, 256], P(('row', 'col'))
- leaf_node: float32 [64, 512, 256], P(('row', 'col'))
- leaf_diag: float32 [64, 256, 256], P(('row', 'col'))
All inputs are finite; a program needn't handle non-finite values. No bound on the sum of `leaf_pattern` on one device may be relied on, other than what follows from the above.
Results may differ from a plain program's by a relative error of at most 0.0001.
Values sent between devices are 32-bit elements; how exact they have to be, the bound alone decides.
A program may use at most 64 MiB of HBM per device.

v0:
```python
import jax
import jax.numpy as jnp
from jax import lax
from jax.sharding import PartitionSpec as P

highest = lax.Precision.HIGHEST


def product(left, right):
    return jnp.matmul(left, right, precision=highest)


def weighted(weights, values):
    return jnp.sum(weights[:, None, None] * values, axis=0)


def shards(
    root_inverse,
    node_factor,
    node_inverse,
    leaf_root_factor,
    leaf_node_factor,
    leaf_inverse,
    leaf_pattern,
    pole_weight,
):
    node_cols = node_factor[:, 0]
    node_inv = node_inverse[:, 0]
    node_leaf = leaf_node_factor[:, 0]
    leaf_inv = leaf_inverse[:, 0]
    block_rows = leaf_root_factor.shape[2] // leaf_pattern.shape[1]
    row_mask = jnp.repeat(leaf_pattern[0].astype(jnp.float32), block_rows)
    root_leaf = leaf_root_factor[:, 0] * row_mask[None, :, None]
    width = node_cols.shape[2]
    joined = jnp.concatenate([node_cols, root_leaf], axis=2)
    products = product(lax.all_gather(root_inverse, ("row", "col"), axis=1, tiled=True), joined)
    offdiag = -products[:, :, :width]
    root_times = products[:, :, width:]
    col_index = lax.axis_index("col")
    own_rows = lax.dynamic_slice_in_dim(node_inv, col_index * width, width, 1)
    factor_t = jnp.swapaxes(node_cols, 1, 2)
    piece = lax.all_gather(offdiag, "col", axis=2, tiled=True)
    root_sum = root_times
    root_sum = root_sum + product(piece, node_leaf)
    node_part = product(jnp.swapaxes(piece, 1, 2), root_leaf)
    cross = product(factor_t, piece)
    root_sum, node_part, cross = (root_sum, node_part, cross)
    diag_rows = own_rows - cross
    diag_times = product(lax.all_gather(diag_rows, "col", axis=1, tiled=True), node_leaf)
    upper_levels = (
        weighted(pole_weight, root_inverse),
        weighted(pole_weight, offdiag)[None],
        weighted(pole_weight, diag_rows)[None],
    )
    middle_part = node_part + diag_times
    lower_part = (
        leaf_inv
        + product(jnp.swapaxes(root_leaf, 1, 2), root_sum)
        + product(jnp.swapaxes(node_leaf, 1, 2), middle_part)
    )
    leaf_levels = (
        weighted(pole_weight, -root_sum)[None],
        weighted(pole_weight, -middle_part)[None],
        weighted(pole_weight, lower_part)[None],
    )
    totals = lax.psum(
        (
            upper_levels[0],
            upper_levels[1],
            upper_levels[2],
            leaf_levels[0],
            leaf_levels[1],
            leaf_levels[2],
        ),
        "pole",
    )
    return (totals[0], totals[1], totals[2], totals[3], totals[4], totals[5])


def solution(mesh):
    return jax.shard_map(
        shards,
        mesh=mesh,
        in_specs=(
            P("pole", ("row", "col"), None),
            P("pole", "row", None, "col"),
            P("pole", "row", None, None),
            P("pole", ("row", "col"), None, None),
            P("pole", ("row", "col"), None, None),
            P("pole", ("row", "col"), None, None),
            P(("row", "col"), None),
            P("pole"),
        ),
        out_specs=(
            P(("row", "col"), None),
            P("row", None, "col"),
            P("row", "col", None),
            P(("row", "col"), None, None),
            P(("row", "col"), None, None),
            P(("row", "col"), None, None),
        ),
        check_vma=False,
    )
```

profile of v0, /device:TPU:1, one launch (start us, length us, event | category | flops | bytes accessed | tf_op | source)
XLA Modules:
  0.0 272.0 jit_solution(6661913665170530114)
XLA Ops:
  7.2 0.0 copy-start
  7.2 0.0 all-gather.4.cloned.1.call-start
  7.2 0.7 all-gather.4.cloned.1.call-update
  7.9 0.0 copy-start.12
  7.9 0.0 all-gather.6.cloned.1.call-start
  8.0 2.9 %copy.20 = f32[2,1,1024,256]{2,3,0,1:T(8,128)} copy(f32[2,1,1024,256]{3,2,1,0:T(8,128)} %param.11) | data formatting | bytes 4194304 | tf_op args[3]
  10.9 0.0 copy-done.12
  10.9 0.1 broadcast_bitcast_fusion
  11.0 1.8 bitcast_multiply_fusion
  12.8 85.2 %all-gather.4.cloned.1.call-done = f32[2,1024,1024]{2,1,0:T(8,128)} async-done(((f32[2,16,1024]{2,1,0:T(8,128)}), f32[2,1024,1024]{2,1,0:T(8,128)}) %all-gather.4.cloned.1.call-update) | async-done | bytes 8388624 | tf_op jit(solution)/shard_map/all_gather | solution.py:36
  98.0 11.3 %fusion.4 = f32[2,1024,320]{1,2,0:T(8,128)S(1)} fusion(f32[2,1024,1024]{2,1,0:T(8,128)} %all-gather.4.cloned.1.call-done, f32[2,1024,256]{1,2,0:T(8,128)S(1)} %bitcast_multiply_fusion, f32[2,1024,64]{1,2,0:T(8,128)} %bitcast.54), kind=kOutput, calls=%fused_computation.7 | convolution fusion | flops 8053719040 | bytes 13631488 | tf_op jit(solution)/shard_map/dot_general | solution.py:10
  109.4 0.0 copy-start.2
  109.4 1.5 copy-done.2
  110.9 0.0 copy-done.11
  110.9 1.6 slice_negate_fusion
  112.5 0.0 all-gather.6.cloned.1.call-update
  112.5 0.0 all-gather.8.cloned.1.call-start
  112.5 0.0 copy-start.6
  112.5 31.9 %all-gather.6.cloned.1.call-done = f32[2,1024,512]{1,2,0:T(8,128)} async-done(((f32[2,1024,64]{1,2,0:T(8,128)}), f32[2,1024,512]{1,2,0:T(8,128)}) %all-gather.6.cloned.1.call-update) | async-done | bytes 4194320 | tf_op jit(solution)/shard_map/all_gather | solution.py:42
  144.5 7.9 %multiply_reduce_fusion.3 = (f32[64,512]{1,0:T(8,128)}, f32[2,64,512]{2,1,0:T(8,128)}) fusion(f32[2]{0:T(128)S(1)} %copy-done.11, f32[2,1024,512]{1,2,0:T(8,128)} %all-gather.6.cloned.1.call-done, f32[2,1,1024,64]{2,3,1,0:T(8,128)} %param.9, f32[2,1,512,512]{3,2,1,0:T(8,128)} %param.10, s32[]{:T(128)S(6)} %select_n.3), kind=kOutput, calls=%fused_computation.23 | convolution fusion | flops 805470208 | bytes 5373964 | tf_op jit(solution)/shard_map/dot_general | solution.py:10
  152.4 0.0 all-gather.8.cloned.1.call-update
  152.4 0.2 all-reduce.3.cloned.1.call-start
  152.6 0.0 copy-done.6
  152.6 0.7 multiply_reduce_fusion.4
  153.3 0.0 copy-done
  153.3 8.0 %multiply_reduce_fusion = (f32[1024,256]{0,1:T(8,128)}, f32[2,1024,256]{1,2,0:T(8,128)S(1)}) fusion(f32[2]{0:T(128)S(1)} %copy-done.11, f32[2,1024,512]{1,2,0:T(8,128)} %all-gather.6.cloned.1.call-done, f32[2,1,512,256]{3,2,1,0:T(8,128)S(1)} %copy-done, f32[2,1024,320]{1,2,0:T(8,128)} %copy-done.2), kind=kOutput, calls=%fused_computation.6 | convolution fusion | flops 3223060480 | bytes 10485768 | tf_op jit(solution)/shard_map/dot_general | solution.py:10
  161.3 0.0 copy-done.4
  161.3 2.9 %convolution_add_fusion.1 = f32[2,256,256]{2,1,0:T(8,128)} fusion(f32[2,1024,256]{1,2,0:T(8,128)S(1)} %bitcast_multiply_fusion, f32[2,1024,256]{1,2,0:T(8,128)S(1)} %get-tuple-element.23, f32[2,1,256,256]{3,2,1,0:T(8,128)S(1)} %copy-done.4), kind=kOutput, calls=%fused_computation.11 | convolution fusion | flops 1610743808 | bytes 5242880 | tf_op jit(solution)/shard_map/dot_general | solution.py:10
  164.2 16.0 %all-gather.8.cloned.1.call-done = f32[2,512,512]{2,1,0:T(8,128)} async-done(((f32[2,64,512]{2,1,0:T(8,128)}), f32[2,512,512]{2,1,0:T(8,128)}) %all-gather.8.cloned.1.call-update) | async-done | bytes 2097168 | tf_op jit(solution)/shard_map/all_gather | solution.py:49
  180.2 3.7 %fusion.12 = f32[2,512,256]{2,1,0:T(8,128)S(1)} fusion(f32[2,512,512]{2,1,0:T(8,128)} %all-gather.8.cloned.1.call-done, f32[2,1,512,256]{3,2,1,0:T(8,128)S(1)} %copy-done), kind=kOutput, calls=%fused_computation.17 | convolution fusion | flops 1610612736 | bytes 4194304 | tf_op jit(solution)/shard_map/dot_general | solution.py:10
  184.0 0.0 copy-done.1
  184.0 0.0 copy-start.3
  184.0 4.7 %multiply_reduce_fusion.1 = (f32[512,256]{1,0:T(8,128)}, f32[2,512,256]{2,1,0:T(8,128)S(1)}) fusion(f32[2]{0:T(128)S(1)} %copy-done.11, f32[2,512,256]{2,1,0:T(8,128)S(1)} %fusion.12, f32[2,1024,512]{1,2,0:T(8,128)S(1)} %copy-done.1, f32[2,1024,256]{1,2,0:T(8,128)S(1)} %bitcast_multiply_fusion), kind=kOutput, calls=%fused_computation.20 | convolution fusion | flops 3222142976 | bytes 8912904 | tf_op jit(solution)/shard_map/dot_general | solution.py:10
  188.6 0.0 copy-done.3
  188.7 2.6 fusion.9
  191.2 0.0 all-reduce.3.cloned.1.call-update
  191.2 68.0 %all-reduce.3.cloned.1.call-done = (f32[16,1024]{1,0:T(8,128)}, f32[1,1024,64]{1,2,0:T(8,128)}, f32[1,64,512]{2,1,0:T(8,128)}, f32[1,1024,256]{1,2,0:T(8,128)}, ...) async-done(((f32[16,1024]{1,0:T(8,128)}, f32[1,1024,64]{1,2,0:T(8,128)}, f32[1,64,512]{2,1,0:T(8,128)}, f32[1,1024,256]{1,2,0:T(8,128)}, f32[1,512,256]{2,1,0:T(8,128)}, ...) | async-done | bytes 2293776 | tf_op jit(solution)/shard_map/psum | solution.py:66
  259.3 2.6 copy.26
  261.9 0.0 copy-done.10
  261.9 0.6 copy.38
  262.6 0.0 copy-done.8
  262.6 0.7 copy.39
  263.3 0.0 copy-done.9
  263.3 0.7 copy.40
  263.9 0.0 copy-done.5
  263.9 0.8 copy.41
  264.7 0.0 copy-done.7
  264.7 0.7 copy.42
  (9 shorter events, 0.0 us)
Async XLA Ops:
  7.2 146.2 %copy-start = (f32[2,1,512,256]{3,2,1,0:T(8,128)S(1)}, f32[2,1,512,256]{3,2,1,0:T(8,128)}, u32[]{:S(2)}) copy-start(f32[2,1,512,256]{3,2,1,0:T(8,128)} %param.12) | copy-start | bytes 3145732
  7.2 90.8 %all-gather.4.cloned.1.call-start = ((), (), s32[]{:S(2)}) async-start(), calls=%async_computation | async-start | bytes 8519680 | tf_op jit(solution)/shard_map/all_gather | solution.py:36
  7.9 3.0 %copy-start.12 = (s32[1,8]{1,0:T(1,128)S(1)}, s32[1,8]{1,0:T(1,128)}, u32[]{:S(2)}) copy-start(s32[1,8]{1,0:T(1,128)} %param.14) | copy-start | bytes 100
  7.9 136.6 %all-gather.6.cloned.1.call-start = ((), (), s32[]{:S(2)}) async-start(), calls=%async_computation.1 | async-start | bytes 4718592 | tf_op jit(solution)/shard_map/all_gather | solution.py:42
  98.0 12.9 %copy-start.11 = (f32[2]{0:T(128)S(1)}, f32[2]{0:T(128)}, u32[]{:S(2)}) copy-start(f32[2]{0:T(128)} %param.15) | copy-start | bytes 28
  109.4 1.5 copy-start.2
  112.5 67.8 %all-gather.8.cloned.1.call-start = ((), (), s32[]{:S(2)}) async-start(), calls=%async_computation.2 | async-start | bytes 2359296 | tf_op jit(solution)/shard_map/all_gather | solution.py:49
  112.5 40.1 %copy-start.6 = (f32[2,16,1024]{2,1,0:T(8,128)S(1)}, f32[2,16,1024]{2,1,0:T(8,128)}, u32[]{:S(2)}) copy-start(f32[2,16,1024]{2,1,0:T(8,128)} %param.8) | copy-start | bytes 393220
  152.4 106.9 %all-reduce.3.cloned.1.call-start = ((), (), s32[]{:S(2)}) async-start(), calls=%async_computation.3 | async-start | bytes 4587520 | tf_op jit(solution)/shard_map/psum | solution.py:66
  153.3 8.0 %copy-start.4 = (f32[2,1,256,256]{3,2,1,0:T(8,128)S(1)}, f32[2,1,256,256]{3,2,1,0:T(8,128)}, u32[]{:S(2)}) copy-start(f32[2,1,256,256]{3,2,1,0:T(8,128)} %param.13) | copy-start | bytes 1572868
  180.2 3.7 %copy-start.1 = (f32[2,1024,512]{1,2,0:T(8,128)S(1)}, f32[2,1024,512]{1,2,0:T(8,128)}, u32[]{:S(2)}) copy-start(f32[2,1024,512]{1,2,0:T(8,128)} %all-gather.6.cloned.1.call-done) | copy-start | bytes 12582916
  184.0 4.7 %copy-start.3 = (f32[2,256,256]{2,1,0:T(8,128)S(1)}, f32[2,256,256]{2,1,0:T(8,128)}, u32[]{:S(2)}) copy-start(f32[2,256,256]{2,1,0:T(8,128)} %convolution_add_fusion.1) | copy-start | bytes 1572868
  259.3 2.6 copy-start.10
  259.3 3.3 %copy-start.8 = (f32[1,1024,64]{1,2,0:T(8,128)S(1)}, f32[1,1024,64]{1,2,0:T(8,128)}, u32[]{:S(2)}) copy-start(f32[1,1024,64]{1,2,0:T(8,128)} %get-tuple-element.27) | copy-start | bytes 786436
  259.3 4.0 %copy-start.9 = (f32[1,64,512]{2,1,0:T(8,128)S(1)}, f32[1,64,512]{2,1,0:T(8,128)}, u32[]{:S(2)}) copy-start(f32[1,64,512]{2,1,0:T(8,128)} %get-tuple-element.28) | copy-start | bytes 393220
  259.3 4.6 %copy-start.5 = (f32[1,512,256]{2,1,0:T(8,128)S(1)}, f32[1,512,256]{2,1,0:T(8,128)}, u32[]{:S(2)}) copy-start(f32[1,512,256]{2,1,0:T(8,128)} %get-tuple-element.30) | copy-start | bytes 1572868
  259.3 5.4 %copy-start.7 = (f32[1,256,256]{2,1,0:T(8,128)S(1)}, f32[1,256,256]{2,1,0:T(8,128)}, u32[]{:S(2)}) copy-start(f32[1,256,256]{2,1,0:T(8,128)} %get-tuple-element.31) | copy-start | bytes 786436
Sparse Core Ops, SparseCore 0:
  10.8 87.1 all-gather.3
  112.6 31.8 all-gather.5
  152.5 27.6 all-gather.7
  191.4 67.8 all-reduce.2
where the time goes:
time: 272 us
  waiting for transfers between devices  202 us (74%)
  matrix products  41 us (15%)
  between operations  13.9 us (5%)
  local copies, waits for them, and re-layouts  10.7 us (4%)
  other arithmetic  4.09 us (2%)
    all_gather x1, waiting for transfers between devices, shards(): lax.all_gather(root_inverse, ('row', 'col'), axis=1, tiled=True)  85.2 us
    psum x1, waiting for transfers between devices, shards(): lax.psum((upper_levels[0], upper_levels[1], upper_levels[2], leaf_levels[...  68 us
    dot_general x7, matrix products, product(): return jnp.matmul(left, right, precision=highest)  41 us
    all_gather x1, waiting for transfers between devices, shards(): piece = lax.all_gather(offdiag, 'col', axis=2, tiled=True)  31.9 us
    all_gather x1, waiting for transfers between devices, shards(): lax.all_gather(diag_rows, 'col', axis=1, tiled=True)  16 us
    unnamed x33, local copies, waits for them, and re-layouts  10.6 us
  transfers between devices with their start and end apart: 4, of which 4 were waited for; matrix products, arithmetic and copies ran while one was open for 6% of the time, Pallas kernels for 0%

commit v1 on v0

--- a/solution.py
+++ b/solution.py
@@ -33,7 +33,15 @@
     root_leaf = leaf_root_factor[:, 0] * row_mask[None, :, None]
     width = node_cols.shape[2]
     joined = jnp.concatenate([node_cols, root_leaf], axis=2)
-    products = product(lax.all_gather(root_inverse, ("row", "col"), axis=1, tiled=True), joined)
+    products = product(
+        jnp.concatenate(
+            lax.all_to_all(
+                jnp.stack([root_inverse] * lax.axis_size(("row", "col"))), ("row", "col"), 0, 0
+            ),
+            axis=1,
+        ),
+        joined,
+    )
     offdiag = -products[:, :, :width]
     root_times = products[:, :, width:]
     col_index = lax.axis_index("col")

time: 272 us -> 388 us (1.43)
  waiting for transfers between devices: 202 us -> 299 us
  starting transfers between devices: 0.34 us -> 13.6 us
  local copies, waits for them, and re-layouts: 10.7 us -> 19.2 us
    all_to_all x0 -> x1, waiting for transfers between devices: none -> 179 us  [shards(): lax.all_to_all(jnp.stack([root_inverse] * lax.axis_size(('row', 'col'))),...]
    all_gather x1 -> x0, waiting for transfers between devices: 85.2 us -> none  [shards(): lax.all_gather(root_inverse, ('row', 'col'), axis=1, tiled=True)]
    all_to_all x0 -> x1, starting transfers between devices: none -> 13.3 us  [shards(): lax.all_to_all(jnp.stack([root_inverse] * lax.axis_size(('row', 'col'))),...]
    another operation x0 -> x1, local copies, waits for them, and re-layouts: none -> 5.29 us  [shards(): jnp.stack([root_inverse] * lax.axis_size(('row', 'col')))]
    reshape x0 -> x1, local copies, waits for them, and re-layouts: none -> 4.29 us  [shards(): jnp.concatenate(lax.all_to_all(jnp.stack([root_inverse] * lax.axis_size((...]
    all_gather x1, waiting for transfers between devices: 31.9 us -> 35.8 us  [shards(): piece = lax.all_gather(offdiag, 'col', axis=2, tiled=True)]
    unnamed x33 -> x37, local copies, waits for them, and re-layouts: 10.6 us -> 9.56 us
  transfers between devices with their start and end apart: 4 -> 4, of which waited for: 4 -> 4; matrix products, arithmetic and copies ran while one was open for 6% -> 4% of each run, Pallas kernels for 0% -> 0%
where the time goes in v1:
time: 388 us
  waiting for transfers between devices  299 us (77%)
  matrix products  38.7 us (10%)
  local copies, waits for them, and re-layouts  19.2 us (5%)
  between operations  13.9 us (4%)
  starting transfers between devices  13.6 us (4%)
  other arithmetic  4.09 us (1%)
    all_to_all x1, waiting for transfers between devices, shards(): lax.all_to_all(jnp.stack([root_inverse] * lax.axis_size(('row', 'col'))),...  179 us
    psum x1, waiting for transfers between devices, shards(): lax.psum((upper_levels[0], upper_levels[1], upper_levels[2], leaf_levels[...  68 us
    dot_general x7, matrix products, product(): return jnp.matmul(left, right, precision=highest)  38.7 us
    all_gather x1, waiting for transfers between devices, shards(): piece = lax.all_gather(offdiag, 'col', axis=2, tiled=True)  35.8 us
    all_gather x1, waiting for transfers between devices, shards(): lax.all_gather(diag_rows, 'col', axis=1, tiled=True)  16.2 us
    all_to_all x1, starting transfers between devices, shards(): lax.all_to_all(jnp.stack([root_inverse] * lax.axis_size(('row', 'col'))),...  13.3 us
    unnamed x37, local copies, waits for them, and re-layouts  9.56 us
  transfers between devices with their start and end apart: 4, of which 4 were waited for; matrix products, arithmetic and copies ran while one was open for 4% of the time, Pallas kernels for 0%

profile of v1, /device:TPU:1, one launch (start us, length us, event | category | flops | bytes accessed | tf_op | source)
XLA Modules:
  0.0 388.2 jit_solution(11563603786192531948)
XLA Ops:
  7.2 0.0 copy-start
  7.2 5.3 %stack.2 = f32[64,2,16,1024]{3,2,1,0:T(8,128)} broadcast(f32[2,16,1024]{2,1,0:T(8,128)} %param.8), dimensions={1,2,3} | broadcast | bytes 8519680 | tf_op jit(solution)/shard_map/stack | solution.py:39
  12.5 13.3 %all-to-all-start = ((f32[64,2,16,1024]{3,2,1,0:T(8,128)}), f32[64,2,16,1024]{3,2,1,0:T(8,128)}, u32[]{:S(2)}, u32[]{:S(2)}) async-start(f32[64,2,16,1024]{3,2,1,0:T(8,128)} %stack.2), calls=%async_computation | async-start | bytes 16777216 | tf_op jit(solution)/shard_map/all_to_all | solution.py:38
  25.8 0.0 copy-start.14
  25.8 0.0 all-gather.3.cloned.1.call-start
  25.9 0.0 copy-done.3
  25.9 1.8 copy.20
  27.7 0.0 copy-done.14
  27.7 0.1 broadcast_bitcast_fusion
  27.8 1.8 bitcast_multiply_fusion
  29.6 178.6 %all-to-all-done = f32[64,2,16,1024]{3,2,1,0:T(8,128)} async-done(((f32[64,2,16,1024]{3,2,1,0:T(8,128)}), f32[64,2,16,1024]{3,2,1,0:T(8,128)}, u32[]{:S(2)}, u32[]{:S(2)}) %all-to-all-start) | async-done | bytes 8388640 | tf_op jit(solution)/shard_map/all_to_all | solution.py:38
  208.2 4.3 %copy.21 = f32[2,64,16,1024]{3,2,1,0:T(8,128)S(1)} copy(f32[2,64,16,1024]{3,2,0,1:T(8,128)} %bitcast.4) | data formatting | bytes 16777216 | tf_op jit(solution)/shard_map/reshape | solution.py:37
  212.5 0.0 copy-done.5
  212.5 0.0 copy-start.13
  212.5 9.0 %fusion.4 = f32[2,1024,320]{1,2,0:T(8,128)S(1)} fusion(f32[2,1024,1024]{2,1,0:T(8,128)S(1)} %bitcast.54, f32[2,1024,256]{1,2,0:T(8,128)S(1)} %bitcast_multiply_fusion, f32[2,1024,64]{1,2,0:T(8,128)S(1)} %bitcast.57), kind=kOutput, calls=%fused_computation.7 | convolution fusion | flops 8053719040 | bytes 13631488 | tf_op jit(solution)/shard_map/dot_general | solution.py:10
  221.5 0.0 copy-start.2
  221.5 1.5 copy-done.2
  223.1 0.0 copy-done.13
  223.1 1.6 slice_negate_fusion
  224.6 0.0 all-gather.3.cloned.1.call-update
  224.7 0.2 all-gather.5.cloned.1.call-start
  224.9 0.0 copy-start.6
  224.9 35.8 %all-gather.3.cloned.1.call-done = f32[2,1024,512]{1,2,0:T(8,128)} async-done(((f32[2,1024,64]{1,2,0:T(8,128)}), f32[2,1024,512]{1,2,0:T(8,128)}) %all-gather.3.cloned.1.call-update) | async-done | bytes 4194320 | tf_op jit(solution)/shard_map/all_gather | solution.py:50
  260.8 7.9 %multiply_reduce_fusion.3 = (f32[64,512]{1,0:T(8,128)}, f32[2,64,512]{2,1,0:T(8,128)}) fusion(f32[2]{0:T(128)S(1)} %copy-done.13, f32[2,1024,512]{1,2,0:T(8,128)} %all-gather.3.cloned.1.call-done, f32[2,1,1024,64]{2,3,1,0:T(8,128)} %param.9, f32[2,1,512,512]{3,2,1,0:T(8,128)} %param.10, s32[]{:T(128)S(6)} %select_n.3), kind=kOutput, calls=%fused_computation.23 | convolution fusion | flops 805470208 | bytes 5373964 | tf_op jit(solution)/shard_map/dot_general | solution.py:10
  268.6 0.0 all-gather.5.cloned.1.call-update
  268.7 0.0 all-reduce.3.cloned.1.call-start
  268.7 0.0 copy-done.6
  268.7 0.7 multiply_reduce_fusion.4
  269.4 0.0 copy-done
  269.4 8.0 %multiply_reduce_fusion = (f32[1024,256]{0,1:T(8,128)}, f32[2,1024,256]{1,2,0:T(8,128)S(1)}) fusion(f32[2]{0:T(128)S(1)} %copy-done.13, f32[2,1024,512]{1,2,0:T(8,128)} %all-gather.3.cloned.1.call-done, f32[2,1,512,256]{3,2,1,0:T(8,128)S(1)} %copy-done, f32[2,1024,320]{1,2,0:T(8,128)} %copy-done.2), kind=kOutput, calls=%fused_computation.6 | convolution fusion | flops 3223060480 | bytes 10485768 | tf_op jit(solution)/shard_map/dot_general | solution.py:10
  277.4 0.0 copy-done.7
  277.4 2.9 convolution_add_fusion.1
  280.3 16.2 %all-gather.5.cloned.1.call-done = f32[2,512,512]{2,1,0:T(8,128)} async-done(((f32[2,64,512]{2,1,0:T(8,128)}), f32[2,512,512]{2,1,0:T(8,128)}) %all-gather.5.cloned.1.call-update) | async-done | bytes 2097168 | tf_op jit(solution)/shard_map/all_gather | solution.py:57
  296.5 3.7 fusion.12
  300.2 0.0 copy-done.1
  300.2 0.0 copy-start.4
  300.2 4.7 %multiply_reduce_fusion.1 = (f32[512,256]{1,0:T(8,128)}, f32[2,512,256]{2,1,0:T(8,128)S(1)}) fusion(f32[2]{0:T(128)S(1)} %copy-done.13, f32[2,512,256]{2,1,0:T(8,128)S(1)} %fusion.12, f32[2,1024,512]{1,2,0:T(8,128)S(1)} %copy-done.1, f32[2,1024,256]{1,2,0:T(8,128)S(1)} %bitcast_multiply_fusion), kind=kOutput, calls=%fused_computation.20 | convolution fusion | flops 3222142976 | bytes 8912904 | tf_op jit(solution)/shard_map/dot_general | solution.py:10
  304.9 0.0 copy-done.4
  304.9 2.6 fusion.9
  307.5 0.0 all-reduce.3.cloned.1.call-update
  307.5 68.0 %all-reduce.3.cloned.1.call-done = (f32[16,1024]{1,0:T(8,128)}, f32[1,1024,64]{1,2,0:T(8,128)}, f32[1,64,512]{2,1,0:T(8,128)}, f32[1,1024,256]{1,2,0:T(8,128)}, ...) async-done(((f32[16,1024]{1,0:T(8,128)}, f32[1,1024,64]{1,2,0:T(8,128)}, f32[1,64,512]{2,1,0:T(8,128)}, f32[1,1024,256]{1,2,0:T(8,128)}, f32[1,512,256]{2,1,0:T(8,128)}, ...) | async-done | bytes 2293776 | tf_op jit(solution)/shard_map/psum | solution.py:74
  375.6 2.6 copy.27
  378.2 0.6 copy.39
  378.8 0.7 copy.40
  379.5 0.7 copy.41
  380.2 0.0 copy-done.8
  380.2 0.8 copy.42
  381.0 0.7 copy.43
  (14 shorter events, 0.0 us)
Async XLA Ops:
  7.2 262.3 %copy-start = (f32[2,1,512,256]{3,2,1,0:T(8,128)S(1)}, f32[2,1,512,256]{3,2,1,0:T(8,128)}, u32[]{:S(2)}) copy-start(f32[2,1,512,256]{3,2,1,0:T(8,128)} %param.12) | copy-start | bytes 3145732
  12.5 13.4 %copy-start.3 = (f32[2,1,1024,256]{3,2,1,0:T(8,128)S(1)}, f32[2,1,1024,256]{3,2,1,0:T(8,128)}, u32[]{:S(2)}) copy-start(f32[2,1,1024,256]{3,2,1,0:T(8,128)} %param.11) | copy-start | bytes 6291460
  12.5 195.7 %all-to-all-start = ((f32[64,2,16,1024]{3,2,1,0:T(8,128)}), f32[64,2,16,1024]{3,2,1,0:T(8,128)}, u32[]{:S(2)}, u32[]{:S(2)}) async-start(f32[64,2,16,1024]{3,2,1,0:T(8,128)} %stack.2), calls=%async_computation | async-start | bytes 16777216 | tf_op jit(solution)/shard_map/all_to_all | solution.py:38
  25.8 1.9 copy-start.14
  25.8 234.9 %all-gather.3.cloned.1.call-start = ((), (), s32[]{:S(2)}) async-start(), calls=%async_computation.1 | async-start | bytes 4718592 | tf_op jit(solution)/shard_map/all_gather | solution.py:50
  208.2 4.3 %copy-start.5 = (f32[2,1,1024,64]{2,3,1,0:T(8,128)S(1)}, f32[2,1,1024,64]{2,3,1,0:T(8,128)}, u32[]{:S(2)}) copy-start(f32[2,1,1024,64]{2,3,1,0:T(8,128)} %param.9) | copy-start | bytes 1572868
  212.5 10.6 %copy-start.13 = (f32[2]{0:T(128)S(1)}, f32[2]{0:T(128)}, u32[]{:S(2)}) copy-start(f32[2]{0:T(128)} %param.15) | copy-start | bytes 28
  221.5 1.5 copy-start.2
  224.7 71.8 %all-gather.5.cloned.1.call-start = ((), (), s32[]{:S(2)}) async-start(), calls=%async_computation.2 | async-start | bytes 2359296 | tf_op jit(solution)/shard_map/all_gather | solution.py:57
  224.9 43.8 %copy-start.6 = (f32[2,16,1024]{2,1,0:T(8,128)S(1)}, f32[2,16,1024]{2,1,0:T(8,128)}, u32[]{:S(2)}) copy-start(f32[2,16,1024]{2,1,0:T(8,128)} %param.8) | copy-start | bytes 393220
  268.7 106.9 %all-reduce.3.cloned.1.call-start = ((), (), s32[]{:S(2)}) async-start(), calls=%async_computation.3 | async-start | bytes 4587520 | tf_op jit(solution)/shard_map/psum | solution.py:74
  269.4 8.0 %copy-start.7 = (f32[2,1,256,256]{3,2,1,0:T(8,128)S(1)}, f32[2,1,256,256]{3,2,1,0:T(8,128)}, u32[]{:S(2)}) copy-start(f32[2,1,256,256]{3,2,1,0:T(8,128)} %param.13) | copy-start | bytes 1572868
  296.5 3.7 copy-start.1
  300.2 4.7 %copy-start.4 = (f32[2,256,256]{2,1,0:T(8,128)S(1)}, f32[2,256,256]{2,1,0:T(8,128)}, u32[]{:S(2)}) copy-start(f32[2,256,256]{2,1,0:T(8,128)} %convolution_add_fusion.1) | copy-start | bytes 1572868
  375.5 2.6 copy-start.12
  375.6 3.3 copy-start.10
  375.6 4.0 %copy-start.11 = (f32[1,64,512]{2,1,0:T(8,128)S(1)}, f32[1,64,512]{2,1,0:T(8,128)}, u32[]{:S(2)}) copy-start(f32[1,64,512]{2,1,0:T(8,128)} %get-tuple-element.28) | copy-start | bytes 393220
  375.6 4.6 %copy-start.8 = (f32[1,512,256]{2,1,0:T(8,128)S(1)}, f32[1,512,256]{2,1,0:T(8,128)}, u32[]{:S(2)}) copy-start(f32[1,512,256]{2,1,0:T(8,128)} %get-tuple-element.30) | copy-start | bytes 1572868
  375.6 5.4 %copy-start.9 = (f32[1,256,256]{2,1,0:T(8,128)S(1)}, f32[1,256,256]{2,1,0:T(8,128)}, u32[]{:S(2)}) copy-start(f32[1,256,256]{2,1,0:T(8,128)} %get-tuple-element.31) | copy-start | bytes 786436
Sparse Core Ops, SparseCore 0:
  224.8 35.9 all-gather.2
  268.8 27.6 all-gather.4
  307.6 67.8 all-reduce.2
